TPU v7x, 256 devices: a whole 4x4x8 slice. The times are simulated.
256 devices in a mesh: seq: 32 (over y, z), tensor: 8 (over x, core).
Axes of the slice: x: 4, y: 4, z: 8, core: 2. Of those that a mesh axis runs over, the one named last changes fastest.
Arguments:
- state: bfloat16 [32768, 2048], P('seq', 'tensor'), may hold values from -20.5 to 20.5
- memory: bfloat16 [512, 2048], P('seq', 'tensor'), may hold values from -20.5 to 20.5
- w_query: bfloat16 [2048, 2048], P('seq', 'tensor'), may hold values from -0.1875 to 0.1875
- w_key: bfloat16 [2048, 2048], P('seq', 'tensor'), may hold values from -0.1875 to 0.1875
- w_value: bfloat16 [2048, 2048], P('seq', 'tensor'), may hold values from -0.125 to 0.125
- w_output: bfloat16 [2048, 2048], P('tensor', 'seq'), may hold values from -0.375 to 0.375
- norm_gain: float32 [2048], P('tensor'), may hold values from 0.1 to 1.9
- remaining: int32 [32768], P('seq'), may hold values from 0 to 3
- slot_home: int32 [512], replicated, may hold values from 0 to 31
Outputs:
- new_state: bfloat16 [32768, 2048], P('seq', 'tensor')
- new_memory: bfloat16 [512, 2048], P('seq', 'tensor')
Inputs may be any that keep to these rules, and one draw needn't show every extreme that they name: `remaining`: 0 means the token has halted.
All inputs are finite; a program needn't handle non-finite values.
Results may differ from a plain program's by a relative error of at most 0.014.
The roundings to bfloat16 on the way count: a program that leaves them out, or rounds other values in their place, can miss the bound.
Values may be sent and summed in bfloat16 or wider, within the bound.
No kernel may reach another device: no remote copies, remote signals or barrier semaphores. Data moves between devices by JAX's collectives and lax.ppermute only.
A program may use at most 128 MiB of HBM per device.

v0:
```python
import math
import jax
import jax.numpy as jnp
from jax import lax
from jax.sharding import PartitionSpec as P

D = 2048
H = 16
HD = 128
HALF = 256
QB = 512
EPS = 1e-05
MASKED = -1e30


def with_halo(array, sides, width):
    for axis, dim in sides:
        peers, length = (lax.axis_size(axis), array.shape[dim])
        up = [(i, (i + 1) % peers) for i in range(peers - 1)]
        down = [(j, i) for i, j in up]
        last = lax.slice_in_dim(array, length - width, length, axis=dim)
        initial = lax.slice_in_dim(array, 0, width, axis=dim)
        before = lax.ppermute(last, axis, up)
        after = lax.ppermute(initial, axis, down)
        array = jnp.concatenate([before, array, after], axis=dim)
    return array


def merged(part, axis, combine):
    gathered = jax.tree.map(lambda a: lax.all_gather(a, axis), part)

    def take(source):
        return jax.tree.map(lambda a: lax.dynamic_index_in_dim(a, source, 0, False), gathered)

    return lax.fori_loop(
        1, lax.axis_size(axis), lambda source, state: combine(state, take(source)), take(0)
    )


def head_slopes(first, amount):
    order = (first + jnp.arange(amount, dtype=jnp.int32)).astype(jnp.float32)
    return 0.25 * 8.0 ** (order / (H - 1))


def shards(state, memory, w_query, w_key, w_value, w_output, norm_gain, remaining, slot_home):
    tok_rows = state.shape[0]
    slot_rows = memory.shape[0]
    seq_count = lax.axis_size("seq")
    seq_place = lax.axis_index("seq")
    tensor_place = lax.axis_index("tensor")
    local_width = w_query.shape[1]
    local_heads = local_width // HD
    total_tokens = tok_rows * seq_count
    score_scale = 1.0 / math.sqrt(HD)
    distance_slopes = head_slopes(tensor_place * local_heads, local_heads)
    homes = slot_home.astype(jnp.float32)
    home_gap = jnp.abs(homes - seq_place.astype(jnp.float32))
    slot_bias = distance_slopes[:, None] * home_gap[None, :]
    state_full, memory_full = (
        lax.all_gather(state, "tensor", axis=1, tiled=True),
        lax.all_gather(memory, "tensor", axis=1, tiled=True),
    )
    rows_full = jnp.concatenate([state_full, memory_full], axis=0)
    pieces = (
        lax.all_gather(w_query, "seq", axis=0, tiled=True),
        lax.all_gather(w_key, "seq", axis=0, tiled=True),
        lax.all_gather(w_value, "seq", axis=0, tiled=True),
    )
    query_acc, key_acc, value_acc = tuple(
        (jnp.dot(rows_full, piece, preferred_element_type=jnp.float32) for piece in pieces)
    )
    query = query_acc.astype(jnp.bfloat16)
    keys = key_acc.astype(jnp.bfloat16)
    values = value_acc.astype(jnp.bfloat16)
    slot_heads = jnp.concatenate([query[tok_rows:], keys[tok_rows:], values[tok_rows:]], axis=1)
    all_slots = lax.all_gather(slot_heads, "seq", axis=0, tiled=True)
    memory_slot_query = all_slots[:, :local_width].reshape(-1, local_heads, HD)
    memory_slot_keys = all_slots[:, local_width : 2 * local_width].reshape(-1, local_heads, HD)
    memory_slot_values = all_slots[:, 2 * local_width :].reshape(-1, local_heads, HD)
    token_key_rows = keys[:tok_rows].reshape(tok_rows, local_heads, HD)
    token_value_rows = values[:tok_rows].reshape(tok_rows, local_heads, HD)
    keys_values = jnp.concatenate([keys[:tok_rows], values[:tok_rows]], axis=1)
    padded = with_halo(keys_values, (("seq", 0),), HALF)
    block = QB
    window_extent = block + 2 * HALF

    def one_block(number):
        start = number * block
        query_matrix = lax.dynamic_slice_in_dim(query, start, block, 0).reshape(
            block, local_heads, HD
        )
        near_rows = lax.dynamic_slice_in_dim(padded, start, window_extent, 0)
        near_keys = near_rows[:, :local_width].reshape(window_extent, local_heads, HD)
        near_values = near_rows[:, local_width:].reshape(window_extent, local_heads, HD)
        near = (
            jnp.einsum("qhd,khd->hqk", query_matrix, near_keys, preferred_element_type=jnp.float32)
            * score_scale
        )
        first = seq_place * tok_rows + start
        qpos = first + jnp.arange(block, dtype=jnp.int32)
        kpos = first - HALF + jnp.arange(window_extent, dtype=jnp.int32)
        valid = (
            (jnp.abs(qpos[:, None] - kpos[None, :]) <= HALF)
            & (kpos >= 0)[None, :]
            & (kpos < total_tokens)[None, :]
        )
        near = jnp.where(valid[None], near, MASKED)
        distant_mask = (
            jnp.einsum(
                "taw,caw->atc", query_matrix, memory_slot_keys, preferred_element_type=jnp.float32
            )
            * score_scale
            - slot_bias[:, None, :]
        )
        scores = jnp.concatenate([near, distant_mask], axis=2)
        top = jnp.max(scores, axis=2, keepdims=True)
        exponent_terms = jnp.exp(scores - top)
        total = jnp.sum(exponent_terms, axis=2)
        attention_probabilities = exponent_terms.astype(jnp.bfloat16)
        numer = jnp.einsum(
            "hqk,khd->qhd",
            attention_probabilities[:, :, :window_extent],
            near_values,
            preferred_element_type=jnp.float32,
        )
        numer = numer + jnp.einsum(
            "lse,elf->slf",
            attention_probabilities[:, :, window_extent:],
            memory_slot_values,
            preferred_element_type=jnp.float32,
        )
        return (
            (numer / jnp.transpose(total)[:, :, None])
            .astype(jnp.bfloat16)
            .reshape(block, local_width)
        )

    token_mix = lax.map(one_block, jnp.arange(tok_rows // block, dtype=jnp.int32)).reshape(
        tok_rows, local_width
    )
    unnormalized_scores = (
        jnp.einsum(
            "gki,pki->kgp", memory_slot_query, token_key_rows, preferred_element_type=jnp.float32
        )
        * score_scale
        - slot_bias[:, :, None]
    )
    local_top = jnp.max(unnormalized_scores, axis=2)
    exponent_terms = jnp.exp(unnormalized_scores - local_top[:, :, None])
    local_sum = jnp.transpose(jnp.sum(exponent_terms, axis=2))
    local_num = jnp.einsum(
        "xzg,gxw->zxw",
        exponent_terms.astype(jnp.bfloat16),
        token_value_rows,
        preferred_element_type=jnp.float32,
    )
    local_top = jnp.transpose(local_top)

    def combine(first_part, second_part):
        top = jnp.maximum(first_part[0], second_part[0])
        weight_first = jnp.exp(first_part[0] - top)
        weight_second = jnp.exp(second_part[0] - top)
        sums = weight_first * first_part[1] + weight_second * second_part[1]
        numers = (
            weight_first[:, :, None] * first_part[2] + weight_second[:, :, None] * second_part[2]
        )
        return (top, sums, numers)

    merged_parts = merged((local_top, local_sum, local_num), "seq", combine)
    own_sum = lax.dynamic_slice_in_dim(merged_parts[1], seq_place * slot_rows, slot_rows, 0)
    own_num = lax.dynamic_slice_in_dim(merged_parts[2], seq_place * slot_rows, slot_rows, 0)
    slot_mix = (own_num / own_sum[:, :, None]).astype(jnp.bfloat16).reshape(slot_rows, local_width)
    mixed = jnp.concatenate([token_mix, slot_mix], axis=0)
    partial_rows = jnp.dot(
        mixed,
        lax.all_gather(w_output, "seq", axis=1, tiled=True),
        preferred_element_type=jnp.float32,
    )
    summed = lax.psum_scatter(
        partial_rows.astype(jnp.bfloat16), "tensor", scatter_dimension=1, tiled=True
    ).astype(jnp.float32)
    residual = jnp.concatenate([state, memory], axis=0).astype(jnp.float32) + summed
    squares = lax.psum(jnp.sum(residual * residual, axis=1), "tensor")
    normed_rows = (residual * lax.rsqrt(squares / D + EPS)[:, None] * norm_gain[None, :]).astype(
        jnp.bfloat16
    )
    new_state = jnp.where((remaining > 0)[:, None], normed_rows[:tok_rows], state)
    new_memory = normed_rows[tok_rows:]
    return (new_state, new_memory)


def solution(mesh):
    placed = (
        P("seq", "tensor"),
        P("seq", "tensor"),
        P("seq", "tensor"),
        P("seq", "tensor"),
        P("seq", "tensor"),
        P("tensor", "seq"),
        P("tensor"),
        P("seq"),
        P(),
    )
    return jax.shard_map(
        shards,
        mesh=mesh,
        in_specs=placed,
        out_specs=(P("seq", "tensor"), P("seq", "tensor")),
        check_vma=False,
    )
```

profile of v0, /device:TPU:1, one launch (start us, length us, event | category | flops | bytes accessed | tf_op | source)
XLA Modules:
  0.0 714.2 jit_solution(8940133622111685820)
XLA Ops:
  10.7 16.0 %all_gather.40 = bf16[16,2048]{1,0:T(8,128)(2,1)S(1)} all-gather(bf16[16,256]{1,0:T(8,128)(2,1)} %param.14), channel_id=1, replica_groups=mesh['seq'=32,'tensor'=8] {'tensor'}, dimensions={1}, use_global_device_ids=true | all-gather | bytes 73728 | tf_op jit(solution)/shard_map/all_gather | solution.py:61
  26.8 25.3 %all-gather.10.cloned.1.call-done = bf16[1024,2048]{1,0:T(8,128)(2,1)} async-done(((bf16[1024,256]{1,0:T(8,128)(2,1)}), bf16[1024,2048]{1,0:T(8,128)(2,1)}) %all-gather.10.cloned.1.call-update) | async-done | bytes 4194320 | tf_op jit(solution)/shard_map/all_gather | solution.py:60
  52.1 4.7 constant_dynamic-update-slice_fusion.2
  57.4 69.1 %all-gather.14.cloned.1.call-done = bf16[2048,256]{1,0:T(8,128)(2,1)} async-done(((bf16[64,256]{1,0:T(8,128)(2,1)}), bf16[2048,256]{1,0:T(8,128)(2,1)}) %all-gather.14.cloned.1.call-update) | async-done | bytes 1048592 | tf_op jit(solution)/shard_map/all_gather | solution.py:67
  126.5 3.8 convolution_convert_fusion.2
  130.4 72.6 %all-gather.12.cloned.1.call-done = bf16[2048,256]{1,0:T(8,128)(2,1)} async-done(((bf16[64,256]{1,0:T(8,128)(2,1)}), bf16[2048,256]{1,0:T(8,128)(2,1)}) %all-gather.12.cloned.1.call-update) | async-done | bytes 1048592 | tf_op jit(solution)/shard_map/all_gather | solution.py:66
  203.0 3.8 convolution_convert_fusion.3
  206.9 72.4 %all-gather.16.cloned.1.call-done = bf16[2048,256]{1,0:T(8,128)(2,1)} async-done(((bf16[64,256]{1,0:T(8,128)(2,1)}), bf16[2048,256]{1,0:T(8,128)(2,1)}) %all-gather.16.cloned.1.call-update) | async-done | bytes 1048592 | tf_op jit(solution)/shard_map/all_gather | solution.py:65
  279.3 3.8 convolution_convert_fusion.1
  284.1 36.9 %all_gather.44 = bf16[512,768]{1,0:T(8,128)(2,1)S(1)} all-gather(bf16[16,768]{1,0:T(8,128)(2,1)S(1)} %pad_maximum_fusion.4), channel_id=1, replica_groups=mesh['seq'=32,'tensor'=8] {'seq'}, dimensions={0}, use_global_device_ids=true | all-gather | bytes 811008 | tf_op jit(solution)/shard_map/all_gather | solution.py:76
  332.0 36.6 %all-gather = f32[16384,2]{0,1:T(2,128)S(1)} all-gather(f32[512,2]{0,1:T(2,128)S(1)} %bitcast.123), channel_id=2, replica_groups=mesh['seq'=32,'tensor'=8] {'seq'}, dimensions={0}, use_global_device_ids=true | all-gather | bytes 135168 | tf_op jit(solution)/shard_map/all_gather | solution.py:30
  371.9 35.7 %all-gather.1 = f32[16384,2]{0,1:T(2,128)S(1)} all-gather(f32[512,2]{0,1:T(2,128)S(1)} %bitcast.126), channel_id=3, replica_groups=mesh['seq'=32,'tensor'=8] {'seq'}, dimensions={0}, use_global_device_ids=true | all-gather | bytes 135168 | tf_op jit(solution)/shard_map/all_gather | solution.py:30
  409.9 22.6 %while.33 = (s32[]{:T(128)}, bf16[2,512,256]{2,1,0:T(8,128)(2,1)}, s32[2]{0:T(128)}, bf16[1536,512]{1,0:T(8,128)(2,1)S(1)}, s32[]{:T(128)}, /*index=5*/bf16[1040...) while((s32[]{:T(128)}, bf16[2,512,256]{2,1,0:T(8,128)(2,1)}, ...), condition=%wide.region_4.5_spmd.clone, body=%wide.region_0.4_spmd.clone.sunk | while | flops 819334656 | bytes 41282024 | solution.py:138
  432.4 48.4 %all-gather.20.cloned.1.call-done = f32[16384,2,128]{0,2,1:T(8,128)} async-done(((f32[512,2,128]{0,2,1:T(8,128)}), f32[16384,2,128]{0,2,1:T(8,128)}) %all-gather.20.cloned.1.call-update) | async-done | bytes 16777232 | tf_op jit(solution)/shard_map/all_gather | solution.py:30
  482.2 25.0 %copy.46 = f32[16384,2,128]{2,1,0:T(2,128)} copy(f32[16384,2,128]{0,2,1:T(8,128)} %all-gather.20.cloned.1.call-done) | data formatting | bytes 33554432 | tf_op jit(solution)/shard_map/while | solution.py:35
  507.1 140.4 %while.32 = (s32[]{:T(128)}, f32[512,2]{0,1:T(2,128)S(1)}, f32[512,2]{0,1:T(2,128)S(1)}, f32[512,2,128]{2,1,0:T(2,128)S(1)}, f32[32,512,2]{1,2,0:T(2,128)S(1)}, ...) while((s32[]{:T(128)}, f32[512,2]{0,1:T(2,128)S(1)}, ...), condition=%wide.region_8.9_spmd, body=%wide.region_7.8_spmd.sunk | while | flops 399365 | bytes 1630351 | solution.py:35
  508.2 3.5 fusion.77
  512.7 3.5 fusion.77
  517.3 3.5 fusion.77
  521.8 3.5 fusion.77
  526.3 3.5 fusion.77
  530.9 3.5 fusion.77
  535.4 3.5 fusion.77
  539.9 3.5 fusion.77
  544.5 3.5 fusion.77
  549.0 3.5 fusion.77
  553.5 3.5 fusion.77
  558.0 3.5 fusion.77
  562.5 3.5 fusion.77
  647.9 4.5 convolution_convert_fusion
  653.1 34.7 %reduce-scatter.2.cloned.1.call-done = bf16[1040,256]{1,0:T(8,128)(2,1)} async-done(((bf16[1040,2048]{1,0:T(8,128)(2,1)}), bf16[1040,256]{1,0:T(8,128)(2,1)}) %reduce-scatter.2.cloned.1.call-update) | async-done | bytes 532496 | tf_op jit(solution)/shard_map/reduce_scatter | solution.py:179
  689.1 15.3 %psum.7 = f32[1040]{0:T(1024)S(1)} all-reduce(f32[1040]{0:T(1024)S(1)} %multiply_reduce_fusion), channel_id=1, replica_groups=mesh['seq'=32,'tensor'=8] {'tensor'}, use_global_device_ids=true, to_apply=%region_11.12 | all-reduce | flops 1040 | bytes 8320 | tf_op jit(solution)/shard_map/psum | solution.py:183
  (249 shorter events, 143.0 us)
Async XLA Ops:
  7.2 44.9 %all-gather.10.cloned.1.call-start = ((), (), s32[]{:S(2)}) async-start(), calls=%async_computation.1 | async-start | bytes 4718592 | tf_op jit(solution)/shard_map/all_gather | solution.py:60
  7.9 118.6 %all-gather.14.cloned.1.call-start = ((), (), s32[]{:S(2)}) async-start(), calls=%async_computation.3 | async-start | bytes 1081344 | tf_op jit(solution)/shard_map/all_gather | solution.py:67
  8.6 194.4 %all-gather.12.cloned.1.call-start = ((), (), s32[]{:S(2)}) async-start(), calls=%async_computation.2 | async-start | bytes 1081344 | tf_op jit(solution)/shard_map/all_gather | solution.py:66
  9.4 270.0 %all-gather.16.cloned.1.call-start = ((), (), s32[]{:S(2)}) async-start(), calls=%async_computation.4 | async-start | bytes 1081344 | tf_op jit(solution)/shard_map/all_gather | solution.py:65
  10.0 470.9 %all-gather.20.cloned.1.call-start = ((), (), s32[]{:S(2)}) async-start(), calls=%async_computation.7 | async-start | bytes 17301504 | tf_op jit(solution)/shard_map/all_gather | solution.py:30
  10.7 46.1 %copy-start.11 = (f32[512]{0:T(512)}, f32[512]{0:T(512)S(1)}, u32[]{:S(2)}) copy-start(f32[512]{0:T(512)S(1)} %subtract_abs_fusion) | copy-start | bytes 6148
  26.7 30.1 %copy-start.14 = (f32[2]{0:T(128)}, f32[2]{0:T(128)S(1)}, u32[]{:S(2)}) copy-start(f32[2]{0:T(128)S(1)} %power_multiply_fusion) | copy-start | bytes 28
  26.8 295.1 %copy-start.13 = (f32[2,512]{1,0:T(2,128)}, f32[2,512]{1,0:T(2,128)S(1)}, u32[]{:S(2)}) copy-start(f32[2,512]{1,0:T(2,128)S(1)} %broadcast_multiply_fusion.1) | copy-start | bytes 12292
  284.1 39.7 %copy-start.8 = (bf16[1024,256]{0,1:T(8,128)(2,1)S(1)}, bf16[1024,256]{0,1:T(8,128)(2,1)}, u32[]{:S(2)}) copy-start(bf16[1024,256]{0,1:T(8,128)(2,1)} %copy.45) | copy-start | bytes 1572868
  321.9 1.9 copy-start
  325.9 322.0 %all-gather.18.cloned.1.call-start = ((), (), s32[]{:S(2)}) async-start(), calls=%async_computation.5 | async-start | bytes 1081344 | tf_op jit(solution)/shard_map/all_gather | solution.py:176
  326.5 361.3 %reduce-scatter.2.cloned.1.call-start = ((), (), s32[]{:S(2)}) async-start(), calls=%async_computation.6 | async-start | bytes 4792320 | tf_op jit(solution)/shard_map/reduce_scatter | solution.py:179
  326.6 81.1 %collective-permute-start = (bf16[256,512]{1,0:T(8,128)(2,1)S(1)}, bf16[256,512]{1,0:T(8,128)(2,1)S(1)}, u32[]{:S(2)}, u32[]{:S(2)}) collective-permute-start(bf16[256,512]{1,0:T(8,128)(2,1)S(1)} %get-tuple-element.403), channel_id=1, source_target_pairs={{0,8},{8,16},{16,24},{24,32},{32,40},{40,48},{48,56},{56,64},{64,7... | collective-permute-start | bytes 786440 | tf_op jit(solution)/shard_map/ppermute | solution.py:23
  329.1 79.2 %collective-permute-start.1 = (bf16[256,512]{1,0:T(8,128)(2,1)S(1)}, bf16[256,512]{1,0:T(8,128)(2,1)}, u32[]{:S(2)}, u32[]{:S(2)}) collective-permute-start(bf16[256,512]{1,0:T(8,128)(2,1)S(1)} %get-tuple-element.404), channel_id=1, source_target_pairs={{8,0},{16,8},{24,16},{32,24},{40,32},{48,40},{56,48},{64,56},{72,6... | collective-permute-start | bytes 786440 | tf_op jit(solution)/shard_map/ppermute | solution.py:24
  407.6 0.7 copy-start.10
  409.9 2.9 copy-start.3
  417.5 1.3 copy-start.1
  417.6 2.1 copy-start.9
  418.8 1.5 copy-start.5
  418.8 2.3 copy-start.4
  420.3 0.8 copy-start.6
  421.1 2.9 copy-start.3
  428.8 1.3 copy-start.1
  428.8 2.1 copy-start.9
  430.1 1.5 copy-start.5
  430.1 2.3 copy-start.4
  431.6 0.8 copy-start.6
  507.1 140.7 %copy-start.7 = (bf16[2,512,256]{2,1,0:T(8,128)(2,1)S(1)}, bf16[2,512,256]{2,1,0:T(8,128)(2,1)}, u32[]{:S(2)}) copy-start(bf16[2,512,256]{2,1,0:T(8,128)(2,1)} %get-tuple-element.294) | copy-start | bytes 1572868
  652.4 0.7 copy-start.15
  652.4 35.4 %copy-start.2 = (bf16[1024,256]{1,0:T(8,128)(2,1)S(1)}, bf16[1024,256]{1,0:T(8,128)(2,1)}, u32[]{:S(2)}) copy-start(bf16[1024,256]{1,0:T(8,128)(2,1)} %param.13) | copy-start | bytes 1572868
  652.4 35.4 %copy-start.12 = (bf16[16,256]{1,0:T(8,128)(2,1)S(1)}, bf16[16,256]{1,0:T(8,128)(2,1)}, u32[]{:S(2)}) copy-start(bf16[16,256]{1,0:T(8,128)(2,1)} %param.14) | copy-start | bytes 24580
  652.4 52.0 %copy-start.16 = (f32[256]{0:T(256)S(1)}, f32[256]{0:T(256)}, u32[]{:S(2)}) copy-start(f32[256]{0:T(256)} %param.19) | copy-start | bytes 3076
Sparse Core Ops, SparseCore 0:
  9.8 42.2 all-gather.9
  54.7 71.8 all-gather.13
  129.1 73.8 all-gather.11
  205.5 73.8 all-gather.15
  326.0 154.7 all-gather.19
  483.3 68.5 all-gather.17
  652.5 35.1 reduce-scatter.1
where the time goes:
time: 718 us; the launch traced here: 714 us
  waiting for transfers between devices  326 us (45%)
  other arithmetic  144 us (20%)
  blocking collectives  141 us (20%)
  local copies, waits for them, and re-layouts  55.6 us (8%)
  matrix products  26.7 us (4%)
  between operations  14.4 us (2%)
    add x31, other arithmetic, combine(): weight_first[:, :, None] * first_part[2]  108 us
    all_gather x1, waiting for transfers between devices, shards(): lax.all_gather(w_key, 'seq', axis=0, tiled=True)  72.6 us
    all_gather x1, waiting for transfers between devices, shards(): lax.all_gather(w_query, 'seq', axis=0, tiled=True)  72.4 us
    all_gather x2, blocking collectives, merged(): gathered = jax.tree.map(lambda a: lax.all_gather(a, axis), part)  72.3 us
    all_gather x1, waiting for transfers between devices, shards(): lax.all_gather(w_value, 'seq', axis=0, tiled=True)  69.1 us
    all_gather x1, waiting for transfers between devices, merged(): gathered = jax.tree.map(lambda a: lax.all_gather(a, axis), part)  48.4 us
    all_gather x1, blocking collectives, shards(): all_slots = lax.all_gather(slot_heads, 'seq', axis=0, tiled=True)  36.9 us
    reduce_scatter x1, waiting for transfers between devices, shards(): lax.psum_scatter(partial_rows.astype(jnp.bfloat16), 'tensor', scatter_dim...  34.7 us
  transfers between devices with their start and end apart: 9, of which 6 were waited for; matrix products, arithmetic and copies ran while one was open for 29% of the time, Pallas kernels for 0%

commit v1 on v0

--- a/solution.py
+++ b/solution.py
@@ -64,7 +64,9 @@
     pieces = (
         lax.all_gather(w_query, "seq", axis=0, tiled=True),
         lax.all_gather(w_key, "seq", axis=0, tiled=True),
-        lax.all_gather(w_value, "seq", axis=0, tiled=True),
+        jnp.concatenate(
+            lax.all_to_all(jnp.stack([w_value] * lax.axis_size("seq")), "seq", 0, 0), axis=0
+        ),
     )
     query_acc, key_acc, value_acc = tuple(
         (jnp.dot(rows_full, piece, preferred_element_type=jnp.float32) for piece in pieces)

time: 718 us -> 642 us (0.89)
  waiting for transfers between devices: 326 us -> 238 us
  starting transfers between devices: 4.04 us -> 16 us
    all_gather x1 -> x0, waiting for transfers between devices: 69.1 us -> none  [shards(): lax.all_gather(w_value, 'seq', axis=0, tiled=True)]
    all_to_all x0 -> x1, starting transfers between devices: none -> 12 us  [shards(): lax.all_to_all(jnp.stack([w_value] * lax.axis_size('seq')), 'seq', 0, 0)]
    all_gather x1, waiting for transfers between devices: 25.3 us -> 13.9 us  [shards(): lax.all_gather(state, 'tensor', axis=1, tiled=True)]
  transfers between devices with their start and end apart: 9 -> 9, of which waited for: 6 -> 5; matrix products, arithmetic and copies ran while one was open for 29% -> 32% of each run, Pallas kernels for 0% -> 0%
where the time goes in v1:
time: 642 us; the launch traced here: 638 us
  waiting for transfers between devices  238 us (37%)
  other arithmetic  144 us (22%)
  blocking collectives  139 us (22%)
  local copies, waits for them, and re-layouts  57.6 us (9%)
  matrix products  26.4 us (4%)
  starting transfers between devices  16 us (2%)
  between operations  14.4 us (2%)
    add x31, other arithmetic, combine(): weight_first[:, :, None] * first_part[2]  108 us
    all_gather x1, waiting for transfers between devices, shards(): lax.all_gather(w_query, 'seq', axis=0, tiled=True)  72.5 us
    all_gather x2, blocking collectives, merged(): gathered = jax.tree.map(lambda a: lax.all_gather(a, axis), part)  72.4 us
    all_gather x1, waiting for transfers between devices, shards(): lax.all_gather(w_key, 'seq', axis=0, tiled=True)  65.6 us
    all_gather x1, waiting for transfers between devices, merged(): gathered = jax.tree.map(lambda a: lax.all_gather(a, axis), part)  48.2 us
    all_gather x1, blocking collectives, shards(): all_slots = lax.all_gather(slot_heads, 'seq', axis=0, tiled=True)  36.9 us
    reduce_scatter x1, waiting for transfers between devices, shards(): lax.psum_scatter(partial_rows.astype(jnp.bfloat16), 'tensor', scatter_dim...  34.6 us
    while x2, local copies, waits for them, and re-layouts, merged(): lax.fori_loop(1, lax.axis_size(axis), lambda source, state: combine(state...  25.2 us
  transfers between devices with their start and end apart: 9, of which 5 were waited for; matrix products, arithmetic and copies ran while one was open for 32% of the time, Pallas kernels for 0%

profile of v1, /device:TPU:1, one launch (start us, length us, event | category | flops | bytes accessed | tf_op | source)
XLA Modules:
  0.0 637.9 jit_solution(959577427608948657)
XLA Ops:
  10.5 12.0 %all-to-all-start = ((bf16[32,64,256]{2,1,0:T(8,128)(2,1)}), bf16[32,64,256]{2,1,0:T(8,128)(2,1)S(1)}, u32[]{:S(2)}, u32[]{:S(2)}) async-start(bf16[32,64,256]{2,1,0:T(8,128)(2,1)} %stack.2), calls=%async_computation | async-start | bytes 2097152 | tf_op jit(solution)/shard_map/all_to_all | solution.py:68
  24.0 14.2 %all_gather.37 = bf16[16,2048]{1,0:T(8,128)(2,1)S(1)} all-gather(bf16[16,256]{1,0:T(8,128)(2,1)} %param.14), channel_id=1, replica_groups=mesh['seq'=32,'tensor'=8] {'tensor'}, dimensions={1}, use_global_device_ids=true | all-gather | bytes 73728 | tf_op jit(solution)/shard_map/all_gather | solution.py:61
  38.3 13.9 %all-gather.9.cloned.1.call-done = bf16[1024,2048]{1,0:T(8,128)(2,1)} async-done(((bf16[1024,256]{1,0:T(8,128)(2,1)}), bf16[1024,2048]{1,0:T(8,128)(2,1)}) %all-gather.9.cloned.1.call-update) | async-done | bytes 4194320 | tf_op jit(solution)/shard_map/all_gather | solution.py:60
  52.3 4.7 constant_dynamic-update-slice_fusion.2
  61.2 65.6 %all-gather.11.cloned.1.call-done = bf16[2048,256]{1,0:T(8,128)(2,1)} async-done(((bf16[64,256]{1,0:T(8,128)(2,1)}), bf16[2048,256]{1,0:T(8,128)(2,1)}) %all-gather.11.cloned.1.call-update) | async-done | bytes 1048592 | tf_op jit(solution)/shard_map/all_gather | solution.py:66
  126.7 3.8 convolution_convert_fusion.3
  130.6 72.5 %all-gather.13.cloned.1.call-done = bf16[2048,256]{1,0:T(8,128)(2,1)} async-done(((bf16[64,256]{1,0:T(8,128)(2,1)}), bf16[2048,256]{1,0:T(8,128)(2,1)}) %all-gather.13.cloned.1.call-update) | async-done | bytes 1048592 | tf_op jit(solution)/shard_map/all_gather | solution.py:65
  203.2 3.8 convolution_convert_fusion.1
  208.0 36.9 %all_gather.40 = bf16[512,768]{1,0:T(8,128)(2,1)S(1)} all-gather(bf16[16,768]{1,0:T(8,128)(2,1)S(1)} %pad_maximum_fusion.4), channel_id=1, replica_groups=mesh['seq'=32,'tensor'=8] {'seq'}, dimensions={0}, use_global_device_ids=true | all-gather | bytes 811008 | tf_op jit(solution)/shard_map/all_gather | solution.py:78
  255.8 36.7 %all-gather = f32[16384,2]{0,1:T(2,128)S(1)} all-gather(f32[512,2]{0,1:T(2,128)S(1)} %bitcast.125), channel_id=2, replica_groups=mesh['seq'=32,'tensor'=8] {'seq'}, dimensions={0}, use_global_device_ids=true | all-gather | bytes 135168 | tf_op jit(solution)/shard_map/all_gather | solution.py:30
  295.8 35.7 %all-gather.1 = f32[16384,2]{0,1:T(2,128)S(1)} all-gather(f32[512,2]{0,1:T(2,128)S(1)} %bitcast.128), channel_id=3, replica_groups=mesh['seq'=32,'tensor'=8] {'seq'}, dimensions={0}, use_global_device_ids=true | all-gather | bytes 135168 | tf_op jit(solution)/shard_map/all_gather | solution.py:30
  333.7 22.7 %while.33 = (s32[]{:T(128)}, bf16[2,512,256]{2,1,0:T(8,128)(2,1)}, s32[2]{0:T(128)}, bf16[1536,512]{1,0:T(8,128)(2,1)S(1)}, s32[]{:T(128)}, /*index=5*/bf16[1040...) while((s32[]{:T(128)}, bf16[2,512,256]{2,1,0:T(8,128)(2,1)}, ...), condition=%wide.region_4.5_spmd.clone, body=%wide.region_0.4_spmd.clone.sunk | while | flops 819334656 | bytes 41282024 | solution.py:140
  356.4 48.2 %all-gather.17.cloned.1.call-done = f32[16384,2,128]{0,2,1:T(8,128)} async-done(((f32[512,2,128]{0,2,1:T(8,128)}), f32[16384,2,128]{0,2,1:T(8,128)}) %all-gather.17.cloned.1.call-update) | async-done | bytes 16777232 | tf_op jit(solution)/shard_map/all_gather | solution.py:30
  406.0 25.0 %copy.46 = f32[16384,2,128]{2,1,0:T(2,128)} copy(f32[16384,2,128]{0,2,1:T(8,128)} %all-gather.17.cloned.1.call-done) | data formatting | bytes 33554432 | tf_op jit(solution)/shard_map/while | solution.py:35
  430.9 140.4 %while.32 = (s32[]{:T(128)}, f32[512,2]{0,1:T(2,128)S(1)}, f32[512,2]{0,1:T(2,128)S(1)}, f32[512,2,128]{2,1,0:T(2,128)S(1)}, f32[32,512,2]{1,2,0:T(2,128)S(1)}, ...) while((s32[]{:T(128)}, f32[512,2]{0,1:T(2,128)S(1)}, ...), condition=%wide.region_8.9_spmd, body=%wide.region_7.8_spmd.sunk | while | flops 399365 | bytes 1630351 | solution.py:35
  432.0 3.5 fusion.77
  436.5 3.5 fusion.77
  441.1 3.5 fusion.77
  445.6 3.5 fusion.77
  450.1 3.5 fusion.77
  454.6 3.5 fusion.77
  459.2 3.5 fusion.77
  463.7 3.5 fusion.77
  468.2 3.5 fusion.77
  472.8 3.5 fusion.77
  477.3 3.5 fusion.77
  481.8 3.5 fusion.77
  486.4 3.5 fusion.77
  490.9 3.5 fusion.77
  571.7 4.5 convolution_convert_fusion
  576.9 34.6 %reduce-scatter.2.cloned.1.call-done = bf16[1040,256]{1,0:T(8,128)(2,1)} async-done(((bf16[1040,2048]{1,0:T(8,128)(2,1)}), bf16[1040,256]{1,0:T(8,128)(2,1)}) %reduce-scatter.2.cloned.1.call-update) | async-done | bytes 532496 | tf_op jit(solution)/shard_map/reduce_scatter | solution.py:181
  612.8 15.4 %psum.7 = f32[1040]{0:T(1024)S(1)} all-reduce(f32[1040]{0:T(1024)S(1)} %multiply_reduce_fusion), channel_id=1, replica_groups=mesh['seq'=32,'tensor'=8] {'tensor'}, use_global_device_ids=true, to_apply=%region_11.12 | all-reduce | flops 1040 | bytes 8320 | tf_op jit(solution)/shard_map/psum | solution.py:185
  (249 shorter events, 144.4 us)
Async XLA Ops:
  7.2 45.1 %all-gather.9.cloned.1.call-start = ((), (), s32[]{:S(2)}) async-start(), calls=%async_computation.2 | async-start | bytes 4718592 | tf_op jit(solution)/shard_map/all_gather | solution.py:60
  7.9 118.8 %all-gather.11.cloned.1.call-start = ((), (), s32[]{:S(2)}) async-start(), calls=%async_computation.3 | async-start | bytes 1081344 | tf_op jit(solution)/shard_map/all_gather | solution.py:66
  10.5 47.1 %all-to-all-start = ((bf16[32,64,256]{2,1,0:T(8,128)(2,1)}), bf16[32,64,256]{2,1,0:T(8,128)(2,1)S(1)}, u32[]{:S(2)}, u32[]{:S(2)}) async-start(bf16[32,64,256]{2,1,0:T(8,128)(2,1)} %stack.2), calls=%async_computation | async-start | bytes 2097152 | tf_op jit(solution)/shard_map/all_to_all | solution.py:68
  22.5 180.7 %all-gather.13.cloned.1.call-start = ((), (), s32[]{:S(2)}) async-start(), calls=%async_computation.4 | async-start | bytes 1081344 | tf_op jit(solution)/shard_map/all_gather | solution.py:65
  23.3 381.4 %all-gather.17.cloned.1.call-start = ((), (), s32[]{:S(2)}) async-start(), calls=%async_computation.7 | async-start | bytes 17301504 | tf_op jit(solution)/shard_map/all_gather | solution.py:30
  24.0 33.0 %copy-start.11 = (f32[512]{0:T(512)}, f32[512]{0:T(512)S(1)}, u32[]{:S(2)}) copy-start(f32[512]{0:T(512)S(1)} %subtract_abs_fusion) | copy-start | bytes 6148
  38.3 18.7 %copy-start.14 = (f32[2]{0:T(128)}, f32[2]{0:T(128)S(1)}, u32[]{:S(2)}) copy-start(f32[2]{0:T(128)S(1)} %power_multiply_fusion) | copy-start | bytes 28
  38.3 207.4 %copy-start.13 = (f32[2,512]{1,0:T(2,128)}, f32[2,512]{1,0:T(2,128)S(1)}, u32[]{:S(2)}) copy-start(f32[2,512]{1,0:T(2,128)S(1)} %broadcast_multiply_fusion.1) | copy-start | bytes 12292
  208.0 39.7 %copy-start.8 = (bf16[1024,256]{0,1:T(8,128)(2,1)S(1)}, bf16[1024,256]{0,1:T(8,128)(2,1)}, u32[]{:S(2)}) copy-start(bf16[1024,256]{0,1:T(8,128)(2,1)} %copy.45) | copy-start | bytes 1572868
  245.8 2.0 copy-start
  249.8 321.9 %all-gather.15.cloned.1.call-start = ((), (), s32[]{:S(2)}) async-start(), calls=%async_computation.5 | async-start | bytes 1081344 | tf_op jit(solution)/shard_map/all_gather | solution.py:178
  250.4 361.1 %reduce-scatter.2.cloned.1.call-start = ((), (), s32[]{:S(2)}) async-start(), calls=%async_computation.6 | async-start | bytes 4792320 | tf_op jit(solution)/shard_map/reduce_scatter | solution.py:181
  250.5 81.0 %collective-permute-start = (bf16[256,512]{1,0:T(8,128)(2,1)S(1)}, bf16[256,512]{1,0:T(8,128)(2,1)S(1)}, u32[]{:S(2)}, u32[]{:S(2)}) collective-permute-start(bf16[256,512]{1,0:T(8,128)(2,1)S(1)} %get-tuple-element.403), channel_id=1, source_target_pairs={{0,8},{8,16},{16,24},{24,32},{32,40},{40,48},{48,56},{56,64},{64,7... | collective-permute-start | bytes 786440 | tf_op jit(solution)/shard_map/ppermute | solution.py:23
  252.9 79.2 %collective-permute-start.1 = (bf16[256,512]{1,0:T(8,128)(2,1)S(1)}, bf16[256,512]{1,0:T(8,128)(2,1)}, u32[]{:S(2)}, u32[]{:S(2)}) collective-permute-start(bf16[256,512]{1,0:T(8,128)(2,1)S(1)} %get-tuple-element.404), channel_id=1, source_target_pairs={{8,0},{16,8},{24,16},{32,24},{40,32},{48,40},{56,48},{64,56},{72,6... | collective-permute-start | bytes 786440 | tf_op jit(solution)/shard_map/ppermute | solution.py:24
  331.5 0.6 copy-start.10
  333.7 2.9 copy-start.3
  341.5 1.3 copy-start.1
  341.5 2.1 copy-start.9
  342.7 1.5 copy-start.5
  342.7 2.3 copy-start.4
  344.2 0.8 copy-start.6
  345.1 2.9 copy-start.3
  352.8 1.3 copy-start.1
  352.8 2.1 copy-start.9
  354.1 1.5 copy-start.5
  354.1 2.3 copy-start.4
  355.6 0.8 copy-start.6
  430.9 140.7 %copy-start.7 = (bf16[2,512,256]{2,1,0:T(8,128)(2,1)S(1)}, bf16[2,512,256]{2,1,0:T(8,128)(2,1)}, u32[]{:S(2)}) copy-start(bf16[2,512,256]{2,1,0:T(8,128)(2,1)} %get-tuple-element.294) | copy-start | bytes 1572868
  576.2 0.7 copy-start.15
  576.2 35.3 %copy-start.2 = (bf16[1024,256]{1,0:T(8,128)(2,1)S(1)}, bf16[1024,256]{1,0:T(8,128)(2,1)}, u32[]{:S(2)}) copy-start(bf16[1024,256]{1,0:T(8,128)(2,1)} %param.13) | copy-start | bytes 1572868
  576.2 35.3 %copy-start.12 = (bf16[16,256]{1,0:T(8,128)(2,1)S(1)}, bf16[16,256]{1,0:T(8,128)(2,1)}, u32[]{:S(2)}) copy-start(bf16[16,256]{1,0:T(8,128)(2,1)} %param.14) | copy-start | bytes 24580
  576.2 52.0 %copy-start.16 = (f32[256]{0:T(256)S(1)}, f32[256]{0:T(256)}, u32[]{:S(2)}) copy-start(f32[256]{0:T(256)} %param.19) | copy-start | bytes 3076
Sparse Core Ops, SparseCore 0:
  9.8 42.4 all-gather.8
  54.8 71.8 all-gather.10
  129.3 73.8 all-gather.12
  249.9 154.7 all-gather.16
  407.1 68.5 all-gather.14
  576.4 35.1 reduce-scatter.1
